TPU v7x, 32 devices: a whole 2x2x4 slice. The times are simulated.
32 devices in a mesh: rep: 2 (over x), seq: 16 (over z, y, core).
Axes of the slice: x: 2, y: 2, z: 4, core: 2. Of those that a mesh axis runs over, the one named last changes fastest.
Arguments:
- projected: bfloat16 [24576, 4096], P(('rep', 'seq')), parts along dimension 0, may hold values from -6 to 6
- history_in: bfloat16 [24576, 1024], P(('rep', 'seq')), parts along dimension 0, may hold values from -6 to 6
- norm_gain: float32 [1024], replicated, may hold values from 0.1 to 1.9
- out_proj: bfloat16 [1024, 1024], replicated, may hold values from -0.1875 to 0.1875
- user_spans: int32 [16], P('rep'), parts along dimension 0, may hold values from 1 to 4, as said below
- user_tails: int32 [16], P('rep'), parts along dimension 0, may hold values from 1 to 768
- cand_emb: bfloat16 [4096, 1024], P(('rep', 'seq')), parts along dimension 0, may hold values from -6 to 6
- cand_user: int32 [4096], P(('rep', 'seq')), parts along dimension 0, may hold values from 0 to 7
- cross_down: bfloat16 [2048, 128], replicated, may hold values from -0.125 to 0.125
- cross_up: bfloat16 [128, 2048], replicated, may hold values from -0.5 to 0.5
- cross_bias: float32 [2048], replicated, may hold values from -4 to 4
- score_weight: float32 [2048], replicated, may hold values from -0.125 to 0.125
Outputs:
- history_out: bfloat16 [24576, 1024], P(('rep', 'seq')), parts along dimension 0
- scores: float32 [4096], P(('rep', 'seq')), parts along dimension 0
There are 2 independent parts, one for each index of `rep`. A program takes and returns all parts, laid end to end along the dimension named above; an argument that names none is the same for every part. Nothing has to cross between parts.
Inputs may be any that keep to these rules, and one draw needn't show every extreme that they name: `user_spans`: users own consecutive segments in order and together own all 16 segments; some user owns exactly 4.
All inputs are finite; a program needn't handle non-finite values.
Results may differ from a plain program's by a relative error of at most 0.0059.
Values may be sent and summed in bfloat16 or wider, within the bound.
A program may use at most 128 MiB of HBM per device.

v0:
```python
import jax
import jax.numpy as jnp
from jax import lax
from jax.sharding import PartitionSpec as P

HEADS = 8


def shifted(x, axis, by):
    peers = lax.axis_size(axis)
    pairs = [(i, i + by) for i in range(peers) if 0 <= i + by < peers]
    return lax.ppermute(x, axis, pairs)


def attend(totals, queries, key_values, weight_mask, score_scale):
    key_count = key_values.shape[0]
    model_width = key_values.shape[1] // 2
    head_count = queries.shape[1]
    key_part = key_values[:, :model_width].reshape(key_count, head_count, -1)
    value_part = key_values[:, model_width:].reshape(key_count, head_count, -1)
    logits = (
        jnp.einsum("qhd,khd->hqk", queries, key_part, preferred_element_type=jnp.float32)
        * score_scale
    )
    weights = (jax.nn.silu(logits) * weight_mask).astype(jnp.bfloat16)
    return totals + jnp.einsum(
        "hqk,khd->qhd", weights, value_part, preferred_element_type=jnp.float32
    )


def body(
    projected,
    history_in,
    norm_gain,
    out_proj,
    user_spans,
    user_tails,
    cand_emb,
    cand_user,
    cross_down,
    cross_up,
    cross_bias,
    score_weight,
):
    row_count, model_width = history_in.shape
    head_size = model_width // HEADS
    score_scale = head_size ** (-0.5)
    devices = lax.axis_size("seq")
    my_index = lax.axis_index("seq")
    span_limit = min(4, devices // 2)
    last_dev = jnp.cumsum(user_spans) - 1
    first_dev = last_dev - user_spans + 1
    device_ids = jnp.arange(devices, dtype=jnp.int32)
    owner_of = jnp.sum((first_dev[None, :] <= device_ids[:, None]).astype(jnp.int32), axis=1) - 1
    is_end = device_ids == last_dev[owner_of]
    valid_rows = jnp.where(is_end, user_tails[owner_of], row_count)
    queries = projected[:, model_width : 2 * model_width].reshape(row_count, HEADS, head_size)
    own_block = projected[:, 2 * model_width :]
    row_ids = jnp.arange(row_count, dtype=jnp.int32)
    causal = (row_ids[None, :] <= row_ids[:, None]).astype(jnp.float32)
    totals = attend(
        jnp.zeros((row_count, HEADS, head_size), jnp.float32),
        queries,
        own_block,
        causal,
        score_scale,
    )

    def add_block(totals, key_values, offset):
        source = my_index - offset
        same_user = (source >= 0) & (owner_of[jnp.maximum(source, 0)] == owner_of[my_index])
        result = lax.cond(
            same_user,
            lambda current: attend(current, queries, key_values, jnp.float32(1.0), score_scale),
            lambda current: current,
            totals,
        )
        return result

    def next_block(offset, loop_state):
        totals, moving = loop_state
        moving = shifted(moving, "seq", 1)
        return (add_block(totals, moving, offset), moving)

    totals, moving = lax.fori_loop(1, span_limit, next_block, (totals, own_block))
    valid_here = valid_rows[my_index]
    row_valid = (row_ids < valid_here).astype(jnp.float32)
    attention = totals.reshape(row_count, model_width) * row_valid[:, None]
    row_mean = jnp.mean(attention, axis=1, keepdims=True)
    centered = attention - row_mean
    row_var = jnp.mean(centered * centered, axis=1, keepdims=True)
    normed = centered * lax.rsqrt(row_var + 1e-06) * norm_gain
    gated = (normed * projected[:, :model_width].astype(jnp.float32)).astype(jnp.bfloat16)
    history_out = (
        jnp.dot(gated, out_proj, preferred_element_type=jnp.float32)
        + history_in.astype(jnp.float32)
    ).astype(jnp.bfloat16)
    last_row = jnp.where(is_end[my_index], valid_here - 1, 0)
    final_row = lax.dynamic_slice_in_dim(history_out, last_row, 1, 0)
    final_row = jnp.where(is_end[my_index], final_row, jnp.zeros_like(final_row))
    user_rows = lax.all_gather(final_row, "seq", axis=0, tiled=True)
    user_count = user_spans.shape[0]
    user_match = cand_user[:, None] == jnp.arange(user_count, dtype=jnp.int32)[None, :]
    cand_dev = jnp.sum(jnp.where(user_match, last_dev[None, :], 0), axis=1)
    selector = (cand_dev[:, None] == device_ids[None, :]).astype(jnp.bfloat16)
    user_part = jnp.dot(selector, user_rows, preferred_element_type=jnp.float32).astype(
        jnp.bfloat16
    )
    crossed_in = jnp.concatenate([user_part, cand_emb], axis=1)
    low_rank = jnp.dot(crossed_in, cross_down, preferred_element_type=jnp.float32).astype(
        jnp.bfloat16
    )
    up_part = jnp.dot(low_rank, cross_up, preferred_element_type=jnp.float32)
    input_float = crossed_in.astype(jnp.float32)
    crossed = input_float * (up_part + cross_bias) + input_float
    scores = jnp.sum(crossed * score_weight, axis=1)
    return (history_out, scores)


def solution(mesh):
    in_specs = (
        P(("rep", "seq"), None),
        P(("rep", "seq"), None),
        P(),
        P(),
        P("rep"),
        P("rep"),
        P(("rep", "seq"), None),
        P(("rep", "seq")),
        P(),
        P(),
        P(),
        P(),
    )
    out_specs = (P(("rep", "seq"), None), P(("rep", "seq")))
    return jax.shard_map(body, mesh=mesh, in_specs=in_specs, out_specs=out_specs, check_vma=False)
```

profile of v0, /device:TPU:7, one launch (start us, length us, event | category | flops | bytes accessed | tf_op | source)
XLA Modules:
  0.0 261.3 jit_solution(10896016889106156357)
XLA Ops:
  0.6 0.0 copy-start
  0.6 1.0 reduce-window.7
  1.6 0.7 subtract_add_fusion
  2.3 0.1 convert_reduce_fusion
  2.4 0.5 copy-done.12
  2.9 0.6 dynamic_slice.28
  3.5 5.7 %fusion.36 = (bf16[768,1024]{1,0:T(8,128)(2,1)}, bf16[768,1024]{1,0:T(8,128)(2,1)}, bf16[768,1024]{1,0:T(8,128)(2,1)}, bf16[768,1024]{1,0:T(8,128)(2,1)}) fusion(bf16[768,4096]{1,0:T(8,128)(2,1)} %param.16), kind=kLoop, calls=%fused_computation.59 | loop fusion | bytes 12582912 | tf_op jit(solution)/shard_map/slice | solution.py:93
  9.2 2.6 copy.56
  11.8 2.7 %copy.57 = bf16[768,1024]{0,1:T(8,128)(2,1)} copy(bf16[768,1024]{1,0:T(8,128)(2,1)} %get-tuple-element.218) | data formatting | bytes 3145728
  14.4 2.6 copy.58
  17.0 1.6 fusion.16
  18.6 12.1 %fusion.17 = f32[768,8,128]{2,0,1:T(8,128)} fusion(bf16[768,8,128]{0,2,1:T(8,128)(2,1)} %bitcast.57, f32[768,768]{1,0:T(8,128)} %fusion.16, bf16[768,8,128]{0,2,1:T(8,128)(2,1)} %bitcast.54, bf16[768,8,128]{0,2,1:T(8,128)(2,1)} %bitcast.56), kind=kOutput, calls=%fused_computation.26 | convolution fusion | flops 2448949248 | bytes 10223616 | tf_op jit(solution)/shard_map/hqk,khd->qhd/dot_general | solution.py:26
  30.7 2.6 copy.47
  33.3 4.0 %slice.26 = bf16[768,2048]{1,0:T(8,128)(2,1)} slice(bf16[768,4096]{1,0:T(8,128)(2,1)} %param.16), slice={[0:768], [2048:4096]} | slice | bytes 6291456 | tf_op jit(solution)/shard_map/slice | solution.py:58
  37.2 4.7 %copy.59 = bf16[768,2048]{0,1:T(8,128)(2,1)} copy(bf16[768,2048]{1,0:T(8,128)(2,1)} %slice.26) | data formatting | bytes 6291456
  42.0 129.2 %while.20 = (s32[]{:T(128)}, f32[768,8,128]{2,0,1:T(8,128)}, bf16[768,2048]{0,1:T(8,128)(2,1)}, s32[]{:T(128)}, s32[16]{0:T(128)S(1)}, /*index=5*/s32[1]{0:T(128)}, bf16[768,8,128]{2,0,1:T(8,128)(2,1)}, s32[]{:T(128)}, s32[]{:T(128)}) while((s32[]{:T(128)}, f32[768,8,128]{2,0,1:T(8,128)}, bf16[768,2048]{0,1:T(8,128)(2,1)}, s32[]{:T(128)}, ...), condition=%wide.region_5.6_spmd, body=%wide.region_2.5_spmd.sunk | while | flops 2445017088 | bytes 36176096 | solution.py:85
  42.0 3.7 %collective-permute-start = (bf16[768,2048]{0,1:T(8,128)(2,1)}, bf16[768,2048]{0,1:T(8,128)(2,1)}, u32[]{:S(2)}, u32[]{:S(2)}) collective-permute-start(bf16[768,2048]{0,1:T(8,128)(2,1)} %get-tuple-element.274), channel_id=1, source_target_pairs={{0,1},{1,2},{2,3},{3,4},{4,5},{5,6},{6,7},{7,8},{8,9},{9,10},{10,1... | collective-permute-start | bytes 9437192 | tf_op jit(solution)/shard_map/while/body/eval_jaxpr/ppermute | solution.py:12
  45.7 0.6 dynamic_slice.34
  47.5 32.7 %collective-permute-done = bf16[768,2048]{0,1:T(8,128)(2,1)} collective-permute-done((bf16[768,2048]{0,1:T(8,128)(2,1)}, bf16[768,2048]{0,1:T(8,128)(2,1)}, u32[]{:S(2)}, u32[]{:S(2)}) %collective-permute-start) | collective-permute-done | bytes 3145760 | tf_op jit(solution)/shard_map/while/body/eval_jaxpr/ppermute | solution.py:12
  80.2 3.8 %copy.75 = bf16[768,2048]{0,1:T(8,128)(2,1)} copy(bf16[768,2048]{0,1:T(8,128)(2,1)} %collective-permute-done) | data formatting | bytes 6291456 | tf_op jit(solution)/shard_map/while
  84.0 5.3 %collective-permute-start = (bf16[768,2048]{0,1:T(8,128)(2,1)}, bf16[768,2048]{0,1:T(8,128)(2,1)}, u32[]{:S(2)}, u32[]{:S(2)}) collective-permute-start(bf16[768,2048]{0,1:T(8,128)(2,1)} %get-tuple-element.274), channel_id=1, source_target_pairs={{0,1},{1,2},{2,3},{3,4},{4,5},{5,6},{6,7},{7,8},{8,9},{9,10},{10,1... | collective-permute-start | bytes 9437192 | tf_op jit(solution)/shard_map/while/body/eval_jaxpr/ppermute | solution.py:12
  89.3 0.6 dynamic_slice.34
  91.1 32.7 %collective-permute-done = bf16[768,2048]{0,1:T(8,128)(2,1)} collective-permute-done((bf16[768,2048]{0,1:T(8,128)(2,1)}, bf16[768,2048]{0,1:T(8,128)(2,1)}, u32[]{:S(2)}, u32[]{:S(2)}) %collective-permute-start) | collective-permute-done | bytes 3145760 | tf_op jit(solution)/shard_map/while/body/eval_jaxpr/ppermute | solution.py:12
  123.8 3.8 %copy.75 = bf16[768,2048]{0,1:T(8,128)(2,1)} copy(bf16[768,2048]{0,1:T(8,128)(2,1)} %collective-permute-done) | data formatting | bytes 6291456 | tf_op jit(solution)/shard_map/while
  127.6 5.3 %collective-permute-start = (bf16[768,2048]{0,1:T(8,128)(2,1)}, bf16[768,2048]{0,1:T(8,128)(2,1)}, u32[]{:S(2)}, u32[]{:S(2)}) collective-permute-start(bf16[768,2048]{0,1:T(8,128)(2,1)} %get-tuple-element.274), channel_id=1, source_target_pairs={{0,1},{1,2},{2,3},{3,4},{4,5},{5,6},{6,7},{7,8},{8,9},{9,10},{10,1... | collective-permute-start | bytes 9437192 | tf_op jit(solution)/shard_map/while/body/eval_jaxpr/ppermute | solution.py:12
  132.9 0.6 dynamic_slice.34
  134.7 32.7 %collective-permute-done = bf16[768,2048]{0,1:T(8,128)(2,1)} collective-permute-done((bf16[768,2048]{0,1:T(8,128)(2,1)}, bf16[768,2048]{0,1:T(8,128)(2,1)}, u32[]{:S(2)}, u32[]{:S(2)}) %collective-permute-start) | collective-permute-done | bytes 3145760 | tf_op jit(solution)/shard_map/while/body/eval_jaxpr/ppermute | solution.py:12
  167.4 3.8 %copy.75 = bf16[768,2048]{0,1:T(8,128)(2,1)} copy(bf16[768,2048]{0,1:T(8,128)(2,1)} %collective-permute-done) | data formatting | bytes 6291456 | tf_op jit(solution)/shard_map/while
  171.2 0.7 gather_fusion
  171.9 0.7 gather_fusion.1
  172.6 0.6 dynamic_slice.29
  173.2 0.9 fusion.29
  174.1 2.2 multiply_reduce_fusion.1
  176.4 0.6 multiply_reduce_fusion
  177.0 3.7 %copy.48 = f32[768,8,128]{0,2,1:T(8,128)} copy(f32[768,8,128]{2,0,1:T(8,128)} %get-tuple-element.178) | data formatting | bytes 6291456 | tf_op jit(solution)/shard_map/while | solution.py:85
  180.7 2.6 copy.60
  183.3 3.2 %fusion.12 = bf16[768,1024]{0,1:T(8,128)(2,1)S(1)} fusion(f32[768,8,128]{0,2,1:T(8,128)} %copy.48, bf16[768,1024]{0,1:T(8,128)(2,1)} %copy.60, f32[1024]{0:T(1024)S(1)} %copy-done.3, f32[768]{0:T(1024)S(1)} %add_rsqrt_fusion, f32[768]{0:T(1024)S(1)} %broadcast_multiply_fusion, f32[768]{0:T(1024)S(1)} %fusion.29), kind=kLoop, calls=%fused_computation.16 | loop fusion | flops 5505024 | bytes 6304768 | tf_op jit(solution)/shard_map/convert_element_type | solution.py:93
  186.5 0.0 copy-start.9
  186.5 0.0 copy-start.5
  186.5 0.0 copy-start.7
  186.5 0.0 copy-start.8
  186.5 3.0 %add_convert_fusion = bf16[768,1024]{1,0:T(8,128)(2,1)} fusion(bf16[768,1024]{1,0:T(8,128)(2,1)S(1)} %copy-done.4, bf16[768,1024]{0,1:T(8,128)(2,1)S(1)} %fusion.12, bf16[1024,1024]{1,0:T(8,128)(2,1)S(1)} %copy-done), kind=kOutput, calls=%fused_computation.17 | convolution fusion | flops 1612972032 | bytes 6815744 | tf_op jit(solution)/shard_map/dot_general | solution.py:95
  190.2 0.6 dynamic_slice.30
  191.4 1.4 fusion.28
  192.8 65.8 %all-gather = bf16[16,1,1024]{2,1,0:T(2,128)(2,1)S(1)} all-gather(bf16[1,1,1024]{2,1,0:T(2,128)(2,1)S(1)} %fusion.28), channel_id=1, replica_groups=mesh['rep'=2,'seq'=16] {'seq'}, dimensions={0}, use_global_device_ids=true | all-gather | bytes 34816 | tf_op jit(solution)/shard_map/all_gather | solution.py:101
  258.6 0.1 select_reduce_fusion
  258.7 0.3 convolution_convert_fusion
  259.0 2.3 fusion.18
  (33 shorter events, 0.1 us)
Async XLA Ops:
  0.6 185.8 %copy-start = (bf16[1024,1024]{1,0:T(8,128)(2,1)S(1)}, bf16[1024,1024]{1,0:T(8,128)(2,1)}, u32[]{:S(2)}) copy-start(bf16[1024,1024]{1,0:T(8,128)(2,1)} %param.19) | copy-start | bytes 6291460
  1.6 7.5 %copy-start.10 = (s32[8,1]{0,1:T(1,128)}, s32[8,1]{0,1:T(1,128)S(1)}, u32[]{:S(2)}) copy-start(s32[8,1]{0,1:T(1,128)S(1)} %reduce-window.7) | copy-start | bytes 100
  2.4 0.5 copy-start.12
  42.0 129.2 %copy-start.13 = (s32[16]{0:T(128)S(1)}, s32[16]{0:T(128)}, u32[]{:S(2)}) copy-start(s32[16]{0:T(128)} %copy-done.12) | copy-start | bytes 196
  42.0 129.2 %copy-start.11 = (s32[8,1]{0,1:T(1,128)S(1)}, s32[8,1]{0,1:T(1,128)}, u32[]{:S(2)}) copy-start(s32[8,1]{0,1:T(1,128)} %copy-done.10) | copy-start | bytes 100
  42.0 129.9 %copy-start.1 = (s32[8]{0:T(128)S(1)}, s32[8]{0:T(128)}, u32[]{:S(2)}) copy-start(s32[8]{0:T(128)} %param.21) | copy-start | bytes 100
  42.0 38.2 %collective-permute-start = (bf16[768,2048]{0,1:T(8,128)(2,1)}, bf16[768,2048]{0,1:T(8,128)(2,1)}, u32[]{:S(2)}, u32[]{:S(2)}) collective-permute-start(bf16[768,2048]{0,1:T(8,128)(2,1)} %get-tuple-element.274), channel_id=1, source_target_pairs={{0,1},{1,2},{2,3},{3,4},{4,5},{5,6},{6,7},{7,8},{8,9},{9,10},{10,1... | collective-permute-start | bytes 9437192 | tf_op jit(solution)/shard_map/while/body/eval_jaxpr/ppermute | solution.py:12
  84.0 39.8 %collective-permute-start = (bf16[768,2048]{0,1:T(8,128)(2,1)}, bf16[768,2048]{0,1:T(8,128)(2,1)}, u32[]{:S(2)}, u32[]{:S(2)}) collective-permute-start(bf16[768,2048]{0,1:T(8,128)(2,1)} %get-tuple-element.274), channel_id=1, source_target_pairs={{0,1},{1,2},{2,3},{3,4},{4,5},{5,6},{6,7},{7,8},{8,9},{9,10},{10,1... | collective-permute-start | bytes 9437192 | tf_op jit(solution)/shard_map/while/body/eval_jaxpr/ppermute | solution.py:12
  127.6 39.8 %collective-permute-start = (bf16[768,2048]{0,1:T(8,128)(2,1)}, bf16[768,2048]{0,1:T(8,128)(2,1)}, u32[]{:S(2)}, u32[]{:S(2)}) collective-permute-start(bf16[768,2048]{0,1:T(8,128)(2,1)} %get-tuple-element.274), channel_id=1, source_target_pairs={{0,1},{1,2},{2,3},{3,4},{4,5},{5,6},{6,7},{7,8},{8,9},{9,10},{10,1... | collective-permute-start | bytes 9437192 | tf_op jit(solution)/shard_map/while/body/eval_jaxpr/ppermute | solution.py:12
  172.5 3.8 %copy-start.2 = (f32[768,8,128]{2,0,1:T(8,128)S(1)}, f32[768,8,128]{2,0,1:T(8,128)}, u32[]{:S(2)}) copy-start(f32[768,8,128]{2,0,1:T(8,128)} %get-tuple-element.178) | copy-start | bytes 9437188
  180.7 2.6 copy-start.3
  183.3 3.2 %copy-start.4 = (bf16[768,1024]{1,0:T(8,128)(2,1)S(1)}, bf16[768,1024]{1,0:T(8,128)(2,1)}, u32[]{:S(2)}) copy-start(bf16[768,1024]{1,0:T(8,128)(2,1)} %param.17) | copy-start | bytes 4718596
  186.5 72.1 %copy-start.9 = (s32[128]{0:T(128)S(1)}, s32[128]{0:T(128)}, u32[]{:S(2)}) copy-start(s32[128]{0:T(128)} %param.23) | copy-start | bytes 1540
  186.5 72.5 %copy-start.5 = (bf16[128,2048]{1,0:T(8,128)(2,1)S(1)}, bf16[128,2048]{1,0:T(8,128)(2,1)}, u32[]{:S(2)}) copy-start(bf16[128,2048]{1,0:T(8,128)(2,1)} %param.25) | copy-start | bytes 1572868
  186.5 72.5 %copy-start.6 = (bf16[2048,128]{1,0:T(8,128)(2,1)S(1)}, bf16[2048,128]{1,0:T(8,128)(2,1)}, u32[]{:S(2)}) copy-start(bf16[2048,128]{1,0:T(8,128)(2,1)} %param.24) | copy-start | bytes 1572868
  186.5 72.5 %copy-start.7 = (f32[2048]{0:T(1024)S(1)}, f32[2048]{0:T(1024)}, u32[]{:S(2)}) copy-start(f32[2048]{0:T(1024)} %param.27) | copy-start | bytes 24580
  186.5 72.5 %copy-start.8 = (f32[2048]{0:T(1024)S(1)}, f32[2048]{0:T(1024)}, u32[]{:S(2)}) copy-start(f32[2048]{0:T(1024)} %param.26) | copy-start | bytes 24580
where the time goes:
time: 262 us; the launch traced here: 261 us
  waiting for transfers between devices  98 us (37%)
  blocking collectives  65.8 us (25%)
  local copies, waits for them, and re-layouts  48 us (18%)
  matrix products  17.6 us (7%)
  starting transfers between devices  14.3 us (5%)
  other arithmetic  11.7 us (4%)
  loops' own time  3.68 us (1%)
    ppermute x3, waiting for transfers between devices, shifted(): return lax.ppermute(x, axis, pairs)  98 us
    all_gather x1, blocking collectives, body(): user_rows = lax.all_gather(final_row, 'seq', axis=0, tiled=True)  65.8 us
    unnamed x33, local copies, waits for them, and re-layouts  15.8 us
    ppermute x3, starting transfers between devices, shifted(): return lax.ppermute(x, axis, pairs)  14.3 us
    dot_general x1, matrix products, attend(): jnp.einsum('hqk,khd->qhd', weights, value_part, preferred_element_type=jn...  12.1 us
    while x3, local copies, waits for them, and re-layouts  11.4 us
    while x2, local copies, waits for them, and re-layouts, body(): lax.fori_loop(1, span_limit, next_block, (totals, own_block))  6.32 us
    slice x1, local copies, waits for them, and re-layouts, body(): projected[:, :model_width].astype(jnp.float32)  5.67 us
  transfers between devices with their start and end apart: 3, of which 3 were waited for; matrix products, arithmetic and copies ran while one was open for 1% of the time, Pallas kernels for 0%

commit v1 on v0

--- a/solution.py
+++ b/solution.py
@@ -98,7 +98,9 @@
     last_row = jnp.where(is_end[my_index], valid_here - 1, 0)
     final_row = lax.dynamic_slice_in_dim(history_out, last_row, 1, 0)
     final_row = jnp.where(is_end[my_index], final_row, jnp.zeros_like(final_row))
-    user_rows = lax.all_gather(final_row, "seq", axis=0, tiled=True)
+    user_rows = jnp.concatenate(
+        lax.all_to_all(jnp.stack([final_row] * lax.axis_size("seq")), "seq", 0, 0), axis=0
+    )
     user_count = user_spans.shape[0]
     user_match = cand_user[:, None] == jnp.arange(user_count, dtype=jnp.int32)[None, :]
     cand_dev = jnp.sum(jnp.where(user_match, last_dev[None, :], 0), axis=1)

time: 262 us -> 254 us (0.969)
  blocking collectives: 65.8 us -> 0 us
  starting transfers between devices: 14.3 us -> 66.9 us
  waiting for transfers between devices: 98 us -> 103 us
    all_gather x1 -> x0, blocking collectives: 65.8 us -> none  [body(): user_rows = lax.all_gather(final_row, 'seq', axis=0, tiled=True)]
    all_to_all x0 -> x1, starting transfers between devices: none -> 52.7 us  [body(): lax.all_to_all(jnp.stack([final_row] * lax.axis_size('seq')), 'seq', 0, 0)]
    all_to_all x0 -> x1, waiting for transfers between devices: none -> 4.95 us  [body(): lax.all_to_all(jnp.stack([final_row] * lax.axis_size('seq')), 'seq', 0, 0)]
    unnamed x33 -> x43, local copies, waits for them, and re-layouts: 15.8 us -> 17.6 us
  transfers between devices with their start and end apart: 3 -> 4, of which waited for: 3 -> 4; matrix products, arithmetic and copies ran while one was open for 1% -> 1% of each run, Pallas kernels for 0% -> 0%
where the time goes in v1:
time: 254 us; the launch traced here: 252 us
  waiting for transfers between devices  103 us (41%)
  starting transfers between devices  66.9 us (26%)
  local copies, waits for them, and re-layouts  48.7 us (19%)
  matrix products  16.5 us (6%)
  other arithmetic  11.3 us (4%)
  loops' own time  3.91 us (2%)
    ppermute x3, waiting for transfers between devices, shifted(): return lax.ppermute(x, axis, pairs)  97.8 us
    all_to_all x1, starting transfers between devices, body(): lax.all_to_all(jnp.stack([final_row] * lax.axis_size('seq')), 'seq', 0, 0)  52.7 us
    unnamed x43, local copies, waits for them, and re-layouts  17.6 us
    ppermute x3, starting transfers between devices, shifted(): return lax.ppermute(x, axis, pairs)  14.3 us
    dot_general x1, matrix products, attend(): jnp.einsum('hqk,khd->qhd', weights, value_part, preferred_element_type=jn...  12.1 us
    while x3, local copies, waits for them, and re-layouts  11.2 us
    slice x1, local copies, waits for them, and re-layouts, body(): projected[:, :model_width].astype(jnp.float32)  6.45 us
    while x2, local copies, waits for them, and re-layouts, body(): lax.fori_loop(1, span_limit, next_block, (totals, own_block))  6.09 us
  transfers between devices with their start and end apart: 4, of which 4 were waited for; matrix products, arithmetic and copies ran while one was open for 1% of the time, Pallas kernels for 0%

profile of v1, /device:TPU:7, one launch (start us, length us, event | category | flops | bytes accessed | tf_op | source)
XLA Modules:
  0.0 252.2 jit_solution(243588154979931169)
XLA Ops:
  0.7 1.6 fusion.16
  2.3 6.5 %fusion.36 = (bf16[768,1024]{1,0:T(8,128)(2,1)}, bf16[768,1024]{1,0:T(8,128)(2,1)}, bf16[768,1024]{1,0:T(8,128)(2,1)}, bf16[768,1024]{1,0:T(8,128)(2,1)}) fusion(bf16[768,4096]{1,0:T(8,128)(2,1)} %param.16), kind=kLoop, calls=%fused_computation.59 | loop fusion | bytes 12582912 | tf_op jit(solution)/shard_map/slice | solution.py:93
  8.8 1.9 slice.26
  10.7 0.2 reduce-window.7
  10.9 0.1 convert_reduce_fusion
  11.0 2.6 %copy.56 = bf16[768,1024]{0,1:T(8,128)(2,1)} copy(bf16[768,1024]{1,0:T(8,128)(2,1)} %get-tuple-element.219) | data formatting | bytes 3145728
  13.6 2.6 %copy.57 = bf16[768,1024]{0,1:T(8,128)(2,1)} copy(bf16[768,1024]{1,0:T(8,128)(2,1)} %get-tuple-element.218) | data formatting | bytes 3145728
  16.2 2.6 %copy.58 = bf16[768,1024]{0,1:T(8,128)(2,1)} copy(bf16[768,1024]{1,0:T(8,128)(2,1)} %get-tuple-element.217) | data formatting | bytes 3145728
  18.8 2.6 %copy.47 = bf16[768,8,128]{2,0,1:T(8,128)(2,1)} copy(bf16[768,8,128]{0,2,1:T(8,128)(2,1)} %bitcast.54) | data formatting | bytes 3145728 | tf_op jit(solution)/shard_map/while | solution.py:85
  21.4 4.6 %copy.59 = bf16[768,2048]{0,1:T(8,128)(2,1)} copy(bf16[768,2048]{1,0:T(8,128)(2,1)} %slice.26) | data formatting | bytes 6291456
  26.0 0.7 gather_fusion
  26.7 0.7 gather_fusion.1
  27.4 0.5 iota_compare_fusion.6
  27.9 0.6 dynamic_slice.28
  28.5 0.6 dynamic_slice.29
  29.1 1.1 fusion.29
  30.2 12.1 %fusion.17 = f32[768,8,128]{2,0,1:T(8,128)} fusion(bf16[768,8,128]{0,2,1:T(8,128)(2,1)} %bitcast.57, f32[768,768]{1,0:T(8,128)} %fusion.16, bf16[768,8,128]{0,2,1:T(8,128)(2,1)} %bitcast.55, bf16[768,8,128]{0,2,1:T(8,128)(2,1)} %bitcast.56), kind=kOutput, calls=%fused_computation.26 | convolution fusion | flops 2448949248 | bytes 10223616 | tf_op jit(solution)/shard_map/hqk,khd->qhd/dot_general | solution.py:26
  42.3 129.0 %while.20 = (s32[]{:T(128)}, f32[768,8,128]{2,0,1:T(8,128)}, bf16[768,2048]{0,1:T(8,128)(2,1)}, s32[]{:T(128)}, s32[16]{0:T(128)S(1)}, /*index=5*/s32[1]{0:T(128)}, bf16[768,8,128]{2,0,1:T(8,128)(2,1)}, s32[]{:T(128)}, s32[]{:T(128)}) while((s32[]{:T(128)}, f32[768,8,128]{2,0,1:T(8,128)}, bf16[768,2048]{0,1:T(8,128)(2,1)}, s32[]{:T(128)}, ...), condition=%wide.region_5.6_spmd, body=%wide.region_2.5_spmd.sunk | while | flops 2445017088 | bytes 36176096 | solution.py:85
  42.3 3.7 %collective-permute-start = (bf16[768,2048]{0,1:T(8,128)(2,1)}, bf16[768,2048]{0,1:T(8,128)(2,1)}, u32[]{:S(2)}, u32[]{:S(2)}) collective-permute-start(bf16[768,2048]{0,1:T(8,128)(2,1)} %get-tuple-element.274), channel_id=1, source_target_pairs={{0,1},{1,2},{2,3},{3,4},{4,5},{5,6},{6,7},{7,8},{8,9},{9,10},{10,1... | collective-permute-start | bytes 9437192 | tf_op jit(solution)/shard_map/while/body/eval_jaxpr/ppermute | solution.py:12
  46.0 0.6 dynamic_slice.34
  47.9 32.6 %collective-permute-done = bf16[768,2048]{0,1:T(8,128)(2,1)} collective-permute-done((bf16[768,2048]{0,1:T(8,128)(2,1)}, bf16[768,2048]{0,1:T(8,128)(2,1)}, u32[]{:S(2)}, u32[]{:S(2)}) %collective-permute-start) | collective-permute-done | bytes 3145760 | tf_op jit(solution)/shard_map/while/body/eval_jaxpr/ppermute | solution.py:12
  80.5 3.7 %copy.75 = bf16[768,2048]{0,1:T(8,128)(2,1)} copy(bf16[768,2048]{0,1:T(8,128)(2,1)} %collective-permute-done) | data formatting | bytes 6291456 | tf_op jit(solution)/shard_map/while
  84.3 5.3 %collective-permute-start = (bf16[768,2048]{0,1:T(8,128)(2,1)}, bf16[768,2048]{0,1:T(8,128)(2,1)}, u32[]{:S(2)}, u32[]{:S(2)}) collective-permute-start(bf16[768,2048]{0,1:T(8,128)(2,1)} %get-tuple-element.274), channel_id=1, source_target_pairs={{0,1},{1,2},{2,3},{3,4},{4,5},{5,6},{6,7},{7,8},{8,9},{9,10},{10,1... | collective-permute-start | bytes 9437192 | tf_op jit(solution)/shard_map/while/body/eval_jaxpr/ppermute | solution.py:12
  89.6 0.6 dynamic_slice.34
  91.5 32.6 %collective-permute-done = bf16[768,2048]{0,1:T(8,128)(2,1)} collective-permute-done((bf16[768,2048]{0,1:T(8,128)(2,1)}, bf16[768,2048]{0,1:T(8,128)(2,1)}, u32[]{:S(2)}, u32[]{:S(2)}) %collective-permute-start) | collective-permute-done | bytes 3145760 | tf_op jit(solution)/shard_map/while/body/eval_jaxpr/ppermute | solution.py:12
  124.1 3.7 %copy.75 = bf16[768,2048]{0,1:T(8,128)(2,1)} copy(bf16[768,2048]{0,1:T(8,128)(2,1)} %collective-permute-done) | data formatting | bytes 6291456 | tf_op jit(solution)/shard_map/while
  127.8 5.3 %collective-permute-start = (bf16[768,2048]{0,1:T(8,128)(2,1)}, bf16[768,2048]{0,1:T(8,128)(2,1)}, u32[]{:S(2)}, u32[]{:S(2)}) collective-permute-start(bf16[768,2048]{0,1:T(8,128)(2,1)} %get-tuple-element.274), channel_id=1, source_target_pairs={{0,1},{1,2},{2,3},{3,4},{4,5},{5,6},{6,7},{7,8},{8,9},{9,10},{10,1... | collective-permute-start | bytes 9437192 | tf_op jit(solution)/shard_map/while/body/eval_jaxpr/ppermute | solution.py:12
  133.1 0.6 dynamic_slice.34
  135.0 32.6 %collective-permute-done = bf16[768,2048]{0,1:T(8,128)(2,1)} collective-permute-done((bf16[768,2048]{0,1:T(8,128)(2,1)}, bf16[768,2048]{0,1:T(8,128)(2,1)}, u32[]{:S(2)}, u32[]{:S(2)}) %collective-permute-start) | collective-permute-done | bytes 3145760 | tf_op jit(solution)/shard_map/while/body/eval_jaxpr/ppermute | solution.py:12
  167.6 3.7 %copy.75 = bf16[768,2048]{0,1:T(8,128)(2,1)} copy(bf16[768,2048]{0,1:T(8,128)(2,1)} %collective-permute-done) | data formatting | bytes 6291456 | tf_op jit(solution)/shard_map/while
  171.3 3.5 %copy.48 = f32[768,8,128]{0,2,1:T(8,128)} copy(f32[768,8,128]{2,0,1:T(8,128)} %get-tuple-element.178) | data formatting | bytes 6291456 | tf_op jit(solution)/shard_map/while | solution.py:85
  174.9 2.4 multiply_reduce_fusion.1
  177.3 0.4 copy-done.4
  177.7 0.6 multiply_reduce_fusion
  178.3 2.8 %copy.60 = bf16[768,1024]{0,1:T(8,128)(2,1)} copy(bf16[768,1024]{1,0:T(8,128)(2,1)} %get-tuple-element.216) | data formatting | bytes 3145728
  181.7 0.6 dynamic_slice.30
  182.9 3.2 %fusion.12 = bf16[768,1024]{0,1:T(8,128)(2,1)S(1)} fusion(f32[768,8,128]{0,2,1:T(8,128)} %copy.48, bf16[768,1024]{0,1:T(8,128)(2,1)} %copy.60, f32[1024]{0:T(1024)S(1)} %copy-done.6, f32[768]{0:T(1024)S(1)} %add_rsqrt_fusion, f32[768]{0:T(1024)S(1)} %broadcast_multiply_fusion, f32[768]{0:T(1024)S(1)} %copy-done.5), kind=kLoop, calls=%fused_computation.16 | loop fusion | flops 5505024 | bytes 6304768 | tf_op jit(solution)/shard_map/convert_element_type | solution.py:93
  186.2 1.8 add_convert_fusion
  188.0 1.1 copy-done.7
  189.2 0.7 fusion.28
  189.9 0.5 broadcast.136
  190.4 0.8 reduce.4
  191.2 0.6 reshape.144
  191.9 52.7 %all-to-all-start = ((bf16[16,2,512]{2,1,0:T(2,128)(2,1)}), bf16[16,2,512]{2,1,0:T(2,128)(2,1)S(1)}, u32[]{:S(2)}, u32[]{:S(2)}) async-start(bf16[16,2,512]{2,1,0:T(2,128)(2,1)} %reshape.144), calls=%async_computation | async-start | bytes 65536 | tf_op jit(solution)/shard_map/all_to_all | solution.py:102
  244.5 0.1 select_reduce_fusion
  244.6 4.9 %all-to-all-done = bf16[16,2,512]{2,1,0:T(2,128)(2,1)S(1)} async-done(((bf16[16,2,512]{2,1,0:T(2,128)(2,1)}), bf16[16,2,512]{2,1,0:T(2,128)(2,1)S(1)}, u32[]{:S(2)}, u32[]{:S(2)}) %all-to-all-start) | async-done | bytes 32800 | tf_op jit(solution)/shard_map/all_to_all | solution.py:102
  249.6 0.3 convolution_convert_fusion
  249.9 2.3 fusion.18
  (48 shorter events, 0.2 us)
Async XLA Ops:
  0.6 185.5 %copy-start = (bf16[1024,1024]{1,0:T(8,128)(2,1)S(1)}, bf16[1024,1024]{1,0:T(8,128)(2,1)}, u32[]{:S(2)}) copy-start(bf16[1024,1024]{1,0:T(8,128)(2,1)} %param.19) | copy-start | bytes 6291460
  0.6 8.1 %slice-start = ((s8[6291456]{0:T(1024)(128)(4,1)}), s8[4194304]{0:T(1024)(128)(4,1)S(1)}, s32[]{:S(2)}) async-start(s8[6291456]{0:T(1024)(128)(4,1)} %bitcast.52), calls=%async_computation.1 | async-start | bytes 8388608
  2.3 6.5 %slice-start.1 = ((s8[6291456]{0:T(1024)(128)(4,1)}), s8[2097152]{0:T(1024)(128)(4,1)S(1)}, s32[]{:S(2)}) async-start(s8[6291456]{0:T(1024)(128)(4,1)} %bitcast.52), calls=%async_computation.2 | async-start | bytes 4194304
  8.7 1.9 copy-start.13
  11.0 15.1 %copy-start.2 = (s32[8]{0:T(128)}, s32[8]{0:T(128)S(1)}, u32[]{:S(2)}) copy-start(s32[8]{0:T(128)S(1)} %add_bitcast_fusion) | copy-start | bytes 100
  21.4 5.3 %copy-start.1 = (s32[8]{0:T(128)S(1)}, s32[8]{0:T(128)}, u32[]{:S(2)}) copy-start(s32[8]{0:T(128)} %param.21) | copy-start | bytes 100
  42.3 38.2 %collective-permute-start = (bf16[768,2048]{0,1:T(8,128)(2,1)}, bf16[768,2048]{0,1:T(8,128)(2,1)}, u32[]{:S(2)}, u32[]{:S(2)}) collective-permute-start(bf16[768,2048]{0,1:T(8,128)(2,1)} %get-tuple-element.274), channel_id=1, source_target_pairs={{0,1},{1,2},{2,3},{3,4},{4,5},{5,6},{6,7},{7,8},{8,9},{9,10},{10,1... | collective-permute-start | bytes 9437192 | tf_op jit(solution)/shard_map/while/body/eval_jaxpr/ppermute | solution.py:12
  84.3 39.8 %collective-permute-start = (bf16[768,2048]{0,1:T(8,128)(2,1)}, bf16[768,2048]{0,1:T(8,128)(2,1)}, u32[]{:S(2)}, u32[]{:S(2)}) collective-permute-start(bf16[768,2048]{0,1:T(8,128)(2,1)} %get-tuple-element.274), channel_id=1, source_target_pairs={{0,1},{1,2},{2,3},{3,4},{4,5},{5,6},{6,7},{7,8},{8,9},{9,10},{10,1... | collective-permute-start | bytes 9437192 | tf_op jit(solution)/shard_map/while/body/eval_jaxpr/ppermute | solution.py:12
  127.8 39.8 %collective-permute-start = (bf16[768,2048]{0,1:T(8,128)(2,1)}, bf16[768,2048]{0,1:T(8,128)(2,1)}, u32[]{:S(2)}, u32[]{:S(2)}) collective-permute-start(bf16[768,2048]{0,1:T(8,128)(2,1)} %get-tuple-element.274), channel_id=1, source_target_pairs={{0,1},{1,2},{2,3},{3,4},{4,5},{5,6},{6,7},{7,8},{8,9},{9,10},{10,1... | collective-permute-start | bytes 9437192 | tf_op jit(solution)/shard_map/while/body/eval_jaxpr/ppermute | solution.py:12
  171.3 3.5 %copy-start.5 = (f32[768]{0:T(1024)S(1)}, f32[768]{0:T(1024)}, u32[]{:S(2)}) copy-start(f32[768]{0:T(1024)} %fusion.29) | copy-start | bytes 9220
  174.9 2.8 %copy-start.4 = (f32[768,8,128]{2,0,1:T(8,128)S(1)}, f32[768,8,128]{2,0,1:T(8,128)}, u32[]{:S(2)}) copy-start(f32[768,8,128]{2,0,1:T(8,128)} %get-tuple-element.178) | copy-start | bytes 9437188
  177.7 4.0 %copy-start.15 = (pred[16]{0:T(512)(128)(4,1)S(1)}, pred[16]{0:T(512)(128)(4,1)}, u32[]{:S(2)}) copy-start(pred[16]{0:T(512)(128)(4,1)} %iota_compare_fusion.6) | copy-start | bytes 52
  177.7 5.2 %copy-start.6 = (f32[1024]{0:T(1024)S(1)}, f32[1024]{0:T(1024)}, u32[]{:S(2)}) copy-start(f32[1024]{0:T(1024)} %param.18) | copy-start | bytes 12292
  182.9 3.2 %copy-start.8 = (bf16[768,1024]{1,0:T(8,128)(2,1)S(1)}, bf16[768,1024]{1,0:T(8,128)(2,1)}, u32[]{:S(2)}) copy-start(bf16[768,1024]{1,0:T(8,128)(2,1)} %param.17) | copy-start | bytes 4718596
  186.1 58.4 %copy-start.3 = (s32[8]{0:T(128)S(1)}, s32[8]{0:T(128)}, u32[]{:S(2)}) copy-start(s32[8]{0:T(128)} %copy-done.2) | copy-start | bytes 100
  186.1 58.4 %copy-start.14 = (s32[128]{0:T(128)S(1)}, s32[128]{0:T(128)}, u32[]{:S(2)}) copy-start(s32[128]{0:T(128)} %param.23) | copy-start | bytes 1540
  186.1 63.7 %copy-start.9 = (bf16[128,2048]{1,0:T(8,128)(2,1)S(1)}, bf16[128,2048]{1,0:T(8,128)(2,1)}, u32[]{:S(2)}) copy-start(bf16[128,2048]{1,0:T(8,128)(2,1)} %param.25) | copy-start | bytes 1572868
  186.2 63.7 %copy-start.10 = (bf16[2048,128]{1,0:T(8,128)(2,1)S(1)}, bf16[2048,128]{1,0:T(8,128)(2,1)}, u32[]{:S(2)}) copy-start(bf16[2048,128]{1,0:T(8,128)(2,1)} %param.24) | copy-start | bytes 1572868
  186.2 63.7 %copy-start.11 = (f32[2048]{0:T(1024)S(1)}, f32[2048]{0:T(1024)}, u32[]{:S(2)}) copy-start(f32[2048]{0:T(1024)} %param.27) | copy-start | bytes 24580
  186.2 63.7 %copy-start.12 = (f32[2048]{0:T(1024)S(1)}, f32[2048]{0:T(1024)}, u32[]{:S(2)}) copy-start(f32[2048]{0:T(1024)} %param.26) | copy-start | bytes 24580
  188.0 1.1 copy-start.7
  191.9 57.7 %all-to-all-start = ((bf16[16,2,512]{2,1,0:T(2,128)(2,1)}), bf16[16,2,512]{2,1,0:T(2,128)(2,1)S(1)}, u32[]{:S(2)}, u32[]{:S(2)}) async-start(bf16[16,2,512]{2,1,0:T(2,128)(2,1)} %reshape.144), calls=%async_computation | async-start | bytes 65536 | tf_op jit(solution)/shard_map/all_to_all | solution.py:102
